TPU v7x, 256 devices: a whole 4x4x8 slice. The times are simulated.
256 devices in a mesh: mem: 16 (over y, x_hi, core), lat: 16 (over z, x_lo).
Axes of the slice: x: 4 (x_hi: 2, x_lo: 2; x = x_hi * 2 + x_lo), y: 4, z: 8, core: 2. Of those that a mesh axis runs over, the one named last changes fastest.
Arguments:
- members: bfloat16 [80, 2, 4, 128, 1152], P('mem', None, None, 'lat'), may hold values from -0.625 to 0.625
- alpha: float32 [80, 4, 128, 1152], P('mem', None, 'lat'), may hold values from -6 to 6
- zonal_loc: bfloat16 [1152, 1152], replicated
- merid_coef: float32 [128, 9], replicated, may hold values from 0.1 to 0.6
- slot_tile: int32 [16, 16, 3], P('lat', 'mem'), may hold values from 0 to 17, as said below
- obs_count: int32 [16, 16, 3], P('lat', 'mem'), may hold values from 0 to 4096, as said below
- obs_index: int32 [16, 16, 3, 4096], P('lat', 'mem'), may hold values from 0 to 16383
- obs_value: float32 [16, 16, 3, 4096], P('lat', 'mem'), may hold values from -6 to 6
- obs_weight: float32 [16, 16, 3, 4096], P('lat', 'mem'), may hold values from 0.5 to 4
Outputs:
- analysis_alpha: float32 [80, 4, 128, 1152], P('mem', None, 'lat')
Inputs may be any that keep to these rules, and one draw needn't show every extreme that they name: `slot_tile`: within each band every tile 0..17 stands in exactly one slot; a device owns at most 3 tiles of a band, and in every band one device owns exactly 3. Unused slots hold tile 0. `obs_count`: zero exactly in unused slots; a used slot holds 4096, 2048 or 1024 live observations, and each band has a slot with 4096.
All inputs are finite; a program needn't handle non-finite values.
Results may differ from a plain program's by a relative error of at most 0.00065.
Values may be sent and summed in bfloat16 or wider, within the bound.
A program may use at most 64 MiB of HBM per device.

v0:
```python
import jax
import jax.numpy as jnp
from jax import lax
from jax.sharding import PartitionSpec as P

TLON = 128
ITERS = 2


step_size = 0.3


def padded_2(cells, sides, width):
    for axis, dim in sides:
        count = lax.axis_size(axis)
        ends = count - 1
        head = lax.slice_in_dim(cells, 0, width, axis=dim)
        tail = lax.slice_in_dim(cells, cells.shape[dim] - width, cells.shape[dim], axis=dim)
        cells = jnp.concatenate(
            [
                lax.ppermute(tail, axis, [(i, (i + 1) % count) for i in range(ends)]),
                cells,
                lax.ppermute(head, axis, [((i + 1) % count, i) for i in range(ends)]),
            ],
            axis=dim,
        )
    return cells


def from_everyone(value, axis):
    count = lax.axis_size(axis)
    return lax.all_to_all(
        jnp.broadcast_to(value[None], (count, *value.shape)), axis, 0, 0, tiled=True
    )


def in_order(blocks, dim):
    blocks = jnp.moveaxis(blocks, 0, dim)
    dims = blocks.shape
    return blocks.reshape(*dims[:dim], dims[dim] * dims[dim + 1], *dims[dim + 2 :])


def collect(value, axis, dim):
    blocks = from_everyone(value, axis)
    return in_order(blocks, dim)


def split_up(value, dim, count):
    before, after = (value.shape[:dim], value.shape[dim + 1 :])
    return jnp.moveaxis(value.reshape(*before, count, -1, *after), dim, 0)


def sum_at_owner(value, axis, dim):
    blocks = split_up(value, dim, lax.axis_size(axis))
    arrived = lax.all_to_all(blocks, axis, split_axis=0, concat_axis=0, tiled=True)
    return arrived.sum(axis=0)


def taken_together(value, axis):
    return from_everyone(value, axis).sum(axis=0)


def meridional(field_pad, coeffs, row_count, half_band):
    running = jnp.zeros(field_pad.shape[:2] + (row_count, field_pad.shape[3]), jnp.float32)
    for offset in range(-half_band, half_band + 1):
        running = (
            running
            + coeffs[:, offset + half_band][None, None, :, None]
            * field_pad[:, :, half_band + offset : half_band + offset + row_count]
        )
    return running


def meridional_back(back_pad, coeffs, row_count, half_band):
    running = jnp.zeros(back_pad.shape[:2] + (row_count, back_pad.shape[3]), jnp.float32)
    for offset in range(-half_band, half_band + 1):
        running = (
            running
            + coeffs[half_band - offset : half_band - offset + row_count, offset + half_band][
                None, None, :, None
            ]
            * back_pad[:, :, half_band - offset : half_band - offset + row_count]
        )
    return running


def fine_tile(coarse):
    inner_rows = coarse.shape[2] - 2
    tile_half = coarse.shape[3] - 1
    even_rows = 0.75 * coarse[:, :, 1:-1] + 0.25 * coarse[:, :, :-2]
    odd_rows = 0.75 * coarse[:, :, 1:-1] + 0.25 * coarse[:, :, 2:]
    merid = jnp.stack([even_rows, odd_rows], axis=3).reshape(
        coarse.shape[0], coarse.shape[1], 2 * inner_rows, coarse.shape[3]
    )
    even_cols = merid[..., :tile_half]
    odd_cols = 0.5 * (merid[..., :tile_half] + merid[..., 1 : tile_half + 1])
    return jnp.stack([even_cols, odd_cols], axis=-1).reshape(
        merid.shape[0], merid.shape[1], merid.shape[2], 2 * tile_half
    )


def tile_windows(field_in, tile_half):
    tile_count = field_in.shape[3] // tile_half
    pieces = field_in.reshape(
        field_in.shape[0], field_in.shape[1], field_in.shape[2], tile_count, tile_half
    )
    following = jnp.roll(pieces[..., :1], -1, axis=3)
    joined = jnp.concatenate([pieces, following], axis=4)
    return joined.transpose(3, 0, 1, 2, 4)


def clamp_poles(field_in, band_index, band_count):
    lower_row = jnp.where(band_index == 0, field_in[:, :, 1], field_in[:, :, 0])
    upper_row = jnp.where(band_index == band_count - 1, field_in[:, :, -2], field_in[:, :, -1])
    return jnp.concatenate(
        [lower_row[:, :, None], field_in[:, :, 1:-1], upper_row[:, :, None]], axis=2
    )


def clamp_back(field_in, band_index, band_count):
    at_south = band_index == 0
    at_north = band_index == band_count - 1
    first_row = jnp.where(at_south, field_in[:, :, 1] + field_in[:, :, 0], field_in[:, :, 1])
    lower_row = jnp.where(at_south, jnp.float32(0.0), field_in[:, :, 0])
    last_row = jnp.where(at_north, field_in[:, :, -2] + field_in[:, :, -1], field_in[:, :, -2])
    upper_row = jnp.where(at_north, jnp.float32(0.0), field_in[:, :, -1])
    return jnp.concatenate(
        [
            lower_row[:, :, None],
            first_row[:, :, None],
            field_in[:, :, 2:-2],
            last_row[:, :, None],
            upper_row[:, :, None],
        ],
        axis=2,
    )


def add_arrived(interior, arrived):
    interior = interior.at[:, :, 0].add(arrived[:, :, 0])
    return interior.at[:, :, -1].add(arrived[:, :, 3])


def body(
    members, alpha, zonal_loc, merid_coef, slot_tile, obs_count, obs_index, obs_value, obs_weight
):
    half_band = merid_coef.shape[1] // 2
    band_rows = alpha.shape[2]
    lon_cells = alpha.shape[3]
    band_index = lax.axis_index("lat")
    band_count = lax.axis_size("lat")
    member_groups = lax.axis_size("mem")
    coef_wide = jnp.pad(merid_coef, ((half_band + 1, half_band + 1), (0, 0)))
    rim_rows = 1
    member_rows = padded_2(members, (("lat", 3),), 1)
    wide_rows = band_rows + 2 * rim_rows
    forward_coef = lax.dynamic_slice_in_dim(
        coef_wide, band_index * band_rows - rim_rows + half_band + 1, wide_rows, 0
    )
    adjoint_coef = lax.dynamic_slice_in_dim(
        coef_wide, band_index * band_rows + 1, band_rows + 2 * half_band, 0
    )
    tile_half = TLON // 2
    tile_ids = slot_tile.reshape(-1)
    live_counts = obs_count.reshape(-1)
    slot_count = tile_ids.shape[0]
    obs_points = obs_index.reshape(slot_count, -1)
    values = obs_value.reshape(slot_count, -1)
    weights = obs_weight.reshape(slot_count, -1)
    slot_obs = obs_points.shape[1]
    owner_table = collect(slot_tile, "mem", 1).reshape(-1)
    current = alpha
    for iteration in range(ITERS):
        padded = padded_2(current, (("lat", 2),), half_band + 1)
        spread = meridional(padded, forward_coef, wide_rows, half_band).astype(jnp.bfloat16)
        zonal_out = jnp.dot(
            spread.reshape(-1, lon_cells), zonal_loc, preferred_element_type=jnp.float32
        ).reshape(spread.shape)
        partial_value = jnp.sum(member_rows * zonal_out[:, None], axis=0)
        chosen = jnp.take(tile_windows(partial_value, tile_half), owner_table, axis=0)
        chosen = chosen.reshape((member_groups, slot_count) + chosen.shape[1:])
        own_windows = sum_at_owner(chosen, "mem", 0)[0]
        adjoint_acc = jnp.zeros(partial_value.shape[:3] + (lon_cells + 1,), jnp.float32)
        for slot_index in range(slot_count):
            col_start = tile_ids[slot_index] * tile_half
            coarse = clamp_poles(own_windows[slot_index], band_index, band_count)
            fine_field, pullback = jax.vjp(fine_tile, coarse)
            flat_tile = fine_field.reshape(-1)
            active = jnp.arange(slot_obs, dtype=jnp.int32) < live_counts[slot_index]
            residual = jnp.where(
                active,
                weights[slot_index] * (flat_tile[obs_points[slot_index]] - values[slot_index]),
                jnp.float32(0.0),
            )
            fine_grad = (
                jnp.zeros(flat_tile.shape, jnp.float32).at[obs_points[slot_index]].add(residual)
            )
            (coarse_grad,) = pullback(fine_grad.reshape(fine_field.shape))
            window = lax.dynamic_slice_in_dim(adjoint_acc, col_start, tile_half + 1, 3)
            adjoint_acc = lax.dynamic_update_slice_in_dim(
                adjoint_acc, window + coarse_grad, col_start, 3
            )
        folded = adjoint_acc[..., :lon_cells].at[..., 0].add(adjoint_acc[..., lon_cells])
        folded = clamp_back(folded, band_index, band_count)
        edge_rows = jnp.stack([folded[:, :, 0], folded[:, :, -1]], axis=2)
        arrived = padded_2(edge_rows, (("lat", 2),), 1)
        adjoint = taken_together(add_arrived(folded[:, :, 1:-1], arrived), "mem")
        weighted = jnp.sum(members * adjoint[None], axis=1).astype(jnp.bfloat16)
        zonal_back = lax.dot_general(
            weighted.reshape(-1, lon_cells),
            zonal_loc,
            (((1,), (1,)), ((), ())),
            preferred_element_type=jnp.float32,
        ).reshape(weighted.shape)
        back_pad = padded_2(zonal_back, (("lat", 2),), half_band)
        gradient = current + meridional_back(back_pad, adjoint_coef, band_rows, half_band)
        current = current - step_size * gradient
    return current


def solution(mesh):
    in_specs = (
        P("mem", None, None, "lat", None),
        P("mem", None, "lat", None),
        P(),
        P(),
        P("lat", "mem", None),
        P("lat", "mem", None),
        P("lat", "mem", None, None),
        P("lat", "mem", None, None),
        P("lat", "mem", None, None),
    )
    out_specs = P("mem", None, "lat", None)
    return jax.shard_map(body, mesh=mesh, in_specs=in_specs, out_specs=out_specs, check_vma=False)
```

profile of v0, /device:TPU:2, one launch (start us, length us, event | category | flops | bytes accessed | tf_op | source)
XLA Modules:
  0.0 794.2 jit_solution(15191835976414677686)
XLA Ops:
  59.9 7.8 all-to-all-start.1
  70.2 25.4 %all-to-all-done.1 = f32[16,1,3,2,4,10,65]{6,4,5,3,2,1,0:T(4,128)} async-done(((f32[16,1,3,2,4,10,65]{6,4,5,3,2,1,0:T(4,128)}), f32[16,1,3,2,4,10,65]{6,4,5,3,2,1,0:T(4,128)}, u32[]{:S(2)}, u32[]{:S(2)}) %all-to-all-start.1) | async-done | bytes 998432 | tf_op jit(solution)/shard_map/all_to_all | solution.py:55
  104.7 23.0 %gather_fusion.2 = f32[4096]{0:T(1024)S(1)} fusion(f32[16384]{0:T(1024)S(1)} %reshape.526, s32[4096]{0:T(1024)S(1)} %copy-done.18), kind=kCustom, calls=%fused_computation.4 | custom fusion | bytes 49152 | tf_op jit(solution)/shard_map/gather | solution.py:192
  128.4 22.1 %scatter_custom_fusion.2 = f32[16384]{0:T(1024)S(1)} fusion(s32[4096]{0:T(1024)} %bitcast.280, f32[4096]{0:T(1024)S(1)} %multiply_select_fusion.3, f32[]{:T(128)} %constant.181.clone.1), kind=kCustom, calls=%fused_computation.372 | custom fusion | flops 4096 | bytes 66048 | tf_op jit(solution)/shard_map/scatter-add | solution.py:196
  156.1 6.8 fusion.3
  171.3 23.0 %gather_fusion.1 = f32[4096]{0:T(1024)S(1)} fusion(f32[16384]{0:T(1024)S(1)} %reshape.523, s32[4096]{0:T(1024)S(1)} %copy-done.16), kind=kCustom, calls=%fused_computation.3 | custom fusion | bytes 49152 | tf_op jit(solution)/shard_map/gather | solution.py:192
  195.0 22.2 %scatter_custom_fusion.1 = f32[16384]{0:T(1024)S(1)} fusion(s32[4096]{0:T(1024)} %bitcast.277, f32[4096]{0:T(1024)S(1)} %multiply_select_fusion.4, f32[]{:T(128)} %constant.181.clone.1), kind=kCustom, calls=%fused_computation.374 | custom fusion | flops 4096 | bytes 66048 | tf_op jit(solution)/shard_map/scatter-add | solution.py:196
  222.8 6.8 fusion.4
  238.1 23.0 %gather_fusion = f32[4096]{0:T(1024)S(1)} fusion(f32[16384]{0:T(1024)S(1)} %reshape.520, s32[4096]{0:T(1024)S(1)} %copy-done.15), kind=kCustom, calls=%fused_computation.2 | custom fusion | bytes 49152 | tf_op jit(solution)/shard_map/gather | solution.py:192
  261.7 22.3 %scatter_custom_fusion = f32[16384]{0:T(1024)S(1)} fusion(s32[4096]{0:T(1024)} %bitcast.274, f32[4096]{0:T(1024)S(1)} %multiply_select_fusion.5, f32[]{:T(128)} %constant.181.clone.1), kind=kCustom, calls=%fused_computation.376 | custom fusion | flops 4096 | bytes 66048 | tf_op jit(solution)/shard_map/scatter-add | solution.py:196
  289.6 6.8 fusion.5
  303.2 8.0 %collective-permute-start.4 = (f32[2,4,1,1152]{3,2,1,0:T(1,128)S(1)}, f32[2,4,1,1152]{3,2,1,0:T(1,128)S(1)}, u32[]{:S(2)}, u32[]{:S(2)}) collective-permute-start(f32[2,4,1,1152]{3,2,1,0:T(1,128)S(1)} %get-tuple-element.108), channel_id=1, source_target_pairs={{0,1},{1,2},{2,3},{3,4},{4,5},{5,6},{6,7},{7,8},{8,9},{9,10},{10,1... | collective-permute-start | bytes 110600 | tf_op jit(solution)/shard_map/ppermute | solution.py:21
  319.7 60.9 %all_to_all.25 = f32[16,2,4,8,1152]{4,3,2,1,0:T(8,128)} all-to-all(f32[16,2,4,8,1152]{4,3,2,1,0:T(8,128)S(1)} %broadcast_in_dim.37), channel_id=1, replica_groups=mesh['mem'=16,'lat'=16] {'mem'}, dimensions={0} | all-to-all | bytes 9437184 | tf_op jit(solution)/shard_map/all_to_all | solution.py:32
  400.9 7.8 collective-permute-done.7
  422.0 17.7 %collective-permute-done.8 = f32[5,4,5,1152]{3,1,2,0:T(4,128)S(1)} collective-permute-done((f32[5,4,5,1152]{3,1,2,0:T(4,128)S(1)}, f32[5,4,5,1152]{3,1,2,0:T(4,128)S(1)}, u32[]{:S(2)}, u32[]{:S(2)}) %collective-permute-start.8) | collective-permute-done | bytes 460832 | tf_op jit(solution)/shard_map/ppermute | solution.py:21
  454.7 31.1 %all_to_all.26 = f32[16,1,3,2,4,10,65]{6,4,5,3,2,1,0:T(4,128)S(1)} all-to-all(f32[16,1,3,2,4,10,65]{6,4,5,3,2,1,0:T(4,128)S(1)} %bitcast.232), channel_id=1, replica_groups=mesh['mem'=16,'lat'=16] {'mem'}, dimensions={0} | all-to-all | bytes 1996800 | tf_op jit(solution)/shard_map/all_to_all | solution.py:55
  493.2 23.0 %gather_fusion.5 = f32[4096]{0:T(1024)S(1)} fusion(f32[16384]{0:T(1024)S(1)} %reshape.536, s32[4096]{0:T(1024)S(1)} %copy-done.19), kind=kCustom, calls=%fused_computation.7 | custom fusion | bytes 49152 | tf_op jit(solution)/shard_map/gather | solution.py:192
  516.9 22.2 %scatter_custom_fusion.5 = f32[16384]{0:T(1024)S(1)} fusion(s32[4096]{0:T(1024)} %bitcast.281, f32[4096]{0:T(1024)S(1)} %multiply_select_fusion, f32[]{:T(128)} %constant.181.clone.1), kind=kCustom, calls=%fused_computation.366 | custom fusion | flops 4096 | bytes 66048 | tf_op jit(solution)/shard_map/scatter-add | solution.py:196
  560.0 23.0 %gather_fusion.4 = f32[4096]{0:T(1024)S(1)} fusion(f32[16384]{0:T(1024)S(1)} %reshape.533, s32[4096]{0:T(1024)S(1)} %copy-done.17), kind=kCustom, calls=%fused_computation.6 | custom fusion | bytes 49152 | tf_op jit(solution)/shard_map/gather | solution.py:192
  583.7 22.3 %scatter_custom_fusion.4 = f32[16384]{0:T(1024)S(1)} fusion(s32[4096]{0:T(1024)} %bitcast.278, f32[4096]{0:T(1024)S(1)} %multiply_select_fusion.1, f32[]{:T(128)} %constant.181.clone.1), kind=kCustom, calls=%fused_computation.368 | custom fusion | flops 4096 | bytes 66048 | tf_op jit(solution)/shard_map/scatter-add | solution.py:196
  626.7 23.0 %gather_fusion.3 = f32[4096]{0:T(1024)S(1)} fusion(f32[16384]{0:T(1024)S(1)} %reshape.530, s32[4096]{0:T(1024)S(1)} %copy-done.15), kind=kCustom, calls=%fused_computation.5 | custom fusion | bytes 49152 | tf_op jit(solution)/shard_map/gather | solution.py:192
  650.4 22.3 %scatter_custom_fusion.3 = f32[16384]{0:T(1024)S(1)} fusion(s32[4096]{0:T(1024)} %bitcast.275, f32[4096]{0:T(1024)S(1)} %multiply_select_fusion.2, f32[]{:T(128)} %constant.181.clone.1), kind=kCustom, calls=%fused_computation.370 | custom fusion | flops 4096 | bytes 66048 | tf_op jit(solution)/shard_map/scatter-add | solution.py:196
  704.7 60.7 %all_to_all.27 = f32[16,2,4,8,1152]{4,3,2,1,0:T(8,128)} all-to-all(f32[16,2,4,8,1152]{4,3,2,1,0:T(8,128)S(1)} %broadcast_in_dim.38), channel_id=1, replica_groups=mesh['mem'=16,'lat'=16] {'mem'}, dimensions={0} | all-to-all | bytes 9437184 | tf_op jit(solution)/shard_map/all_to_all | solution.py:32
  783.8 7.8 collective-permute-done.13
  (360 shorter events, 270.8 us)
Async XLA Ops:
  0.0 44.0 %copy-start = (bf16[1152,1152]{1,0:T(8,128)(2,1)S(1)}, bf16[1152,1152]{1,0:T(8,128)(2,1)}, u32[]{:S(2)}) copy-start(bf16[1152,1152]{1,0:T(8,128)(2,1)} %param.25) | copy-start | bytes 7962628
  2.5 40.4 %collective-permute-start.3 = (f32[5,4,5,1152]{3,1,2,0:T(4,128)}, f32[5,4,5,1152]{3,1,2,0:T(4,128)}, u32[]{:S(2)}, u32[]{:S(2)}) collective-permute-start(f32[5,4,5,1152]{3,1,2,0:T(4,128)} %copy.225), channel_id=1, source_target_pairs={{1,0},{2,1},{3,2},{4,3},{5,4},{6,5},{7,6},{8,7},{9,8},{10,9},{11,1... | collective-permute-start | bytes 1382408 | tf_op jit(solution)/shard_map/ppermute | solution.py:23
  7.7 34.0 %collective-permute-start.2 = (f32[5,4,5,1152]{3,1,2,0:T(4,128)}, f32[5,4,5,1152]{3,1,2,0:T(4,128)}, u32[]{:S(2)}, u32[]{:S(2)}) collective-permute-start(f32[5,4,5,1152]{3,1,2,0:T(4,128)} %copy.224), channel_id=1, source_target_pairs={{0,1},{1,2},{2,3},{3,4},{4,5},{5,6},{6,7},{7,8},{8,9},{9,10},{10,1... | collective-permute-start | bytes 1382408 | tf_op jit(solution)/shard_map/ppermute | solution.py:21
  10.6 28.7 %collective-permute-start = (bf16[5,2,4,1,1152]{4,0,3,2,1:T(8,128)(2,1)S(1)}, bf16[5,2,4,1,1152]{4,0,3,2,1:T(8,128)(2,1)}, u32[]{:S(2)}, u32[]{:S(2)}) collective-permute-start(bf16[5,2,4,1,1152]{4,0,3,2,1:T(8,128)(2,1)S(1)} %copy.222), channel_id=1, source_target_pairs={{0,1},{1,2},{2,3},{3,4},{4,5},{5,6},{6,7},{7,8},{8,9},{9,10},{10,1... | collective-permute-start | bytes 276488 | tf_op jit(solution)/shard_map/ppermute | solution.py:21
  14.2 26.2 %collective-permute-start.1 = (bf16[5,2,4,1,1152]{4,0,3,2,1:T(8,128)(2,1)}, bf16[5,2,4,1,1152]{4,0,3,2,1:T(8,128)(2,1)}, u32[]{:S(2)}, u32[]{:S(2)}) collective-permute-start(bf16[5,2,4,1,1152]{4,0,3,2,1:T(8,128)(2,1)} %copy.223), channel_id=1, source_target_pairs={{1,0},{2,1},{3,2},{4,3},{5,4},{6,5},{7,6},{8,7},{9,8},{10,9},{11,1... | collective-permute-start | bytes 276488 | tf_op jit(solution)/shard_map/ppermute | solution.py:23
  18.4 14.6 %all-to-all-start = ((s32[16,1,1,3]{3,2,1,0:T(1,128)}), s32[16,1,1,3]{3,2,1,0:T(1,128)}, u32[]{:S(2)}, u32[]{:S(2)}) async-start(s32[16,1,1,3]{3,2,1,0:T(1,128)} %broadcast_in_dim.34), calls=%async_computation | async-start | bytes 16384 | tf_op jit(solution)/shard_map/all_to_all | solution.py:32
  59.9 35.8 %all-to-all-start.1 = ((f32[16,1,3,2,4,10,65]{6,4,5,3,2,1,0:T(4,128)}), f32[16,1,3,2,4,10,65]{6,4,5,3,2,1,0:T(4,128)}, u32[]{:S(2)}, u32[]{:S(2)}) async-start(f32[16,1,3,2,4,10,65]{6,4,5,3,2,1,0:T(4,128)} %bitcast.231), calls=%async_computation.1 | async-start | bytes 3932160 | tf_op jit(solution)/shard_map/all_to_all | solution.py:55
  104.7 23.1 %copy-start.14 = (f32[1,1,1,4096]{3,1,2,0:T(1,128)S(1)}, f32[1,1,1,4096]{3,1,2,0:T(1,128)}, u32[]{:S(2)}) copy-start(f32[1,1,1,4096]{3,1,2,0:T(1,128)} %get-tuple-element.146) | copy-start | bytes 49156
  171.3 23.1 %copy-start.13 = (f32[1,1,1,4096]{3,1,2,0:T(1,128)S(1)}, f32[1,1,1,4096]{3,1,2,0:T(1,128)}, u32[]{:S(2)}) copy-start(f32[1,1,1,4096]{3,1,2,0:T(1,128)} %get-tuple-element.148) | copy-start | bytes 49156
  303.2 10.9 %collective-permute-start.4 = (f32[2,4,1,1152]{3,2,1,0:T(1,128)S(1)}, f32[2,4,1,1152]{3,2,1,0:T(1,128)S(1)}, u32[]{:S(2)}, u32[]{:S(2)}) collective-permute-start(f32[2,4,1,1152]{3,2,1,0:T(1,128)S(1)} %get-tuple-element.108), channel_id=1, source_target_pairs={{0,1},{1,2},{2,3},{3,4},{4,5},{5,6},{6,7},{7,8},{8,9},{9,10},{10,1... | collective-permute-start | bytes 110600 | tf_op jit(solution)/shard_map/ppermute | solution.py:21
  312.2 6.8 collective-permute-start.5
  387.9 12.9 %collective-permute-start.6 = (f32[5,4,4,1152]{3,2,1,0:T(4,128)}, f32[5,4,4,1152]{3,2,1,0:T(4,128)}, u32[]{:S(2)}, u32[]{:S(2)}) collective-permute-start(f32[5,4,4,1152]{3,2,1,0:T(4,128)} %get-tuple-element.98), channel_id=1, source_target_pairs={{1,0},{2,1},{3,2},{4,3},{5,4},{6,5},{7,6},{8,7},{9,8},{10,9},{11,1... | collective-permute-start | bytes 1105928 | tf_op jit(solution)/shard_map/ppermute | solution.py:23
  389.9 18.8 %collective-permute-start.7 = (f32[5,4,4,1152]{3,2,1,0:T(4,128)}, f32[5,4,4,1152]{3,2,1,0:T(4,128)}, u32[]{:S(2)}, u32[]{:S(2)}) collective-permute-start(f32[5,4,4,1152]{3,2,1,0:T(4,128)} %get-tuple-element.99), channel_id=1, source_target_pairs={{0,1},{1,2},{2,3},{3,4},{4,5},{5,6},{6,7},{7,8},{8,9},{9,10},{10,1... | collective-permute-start | bytes 1105928 | tf_op jit(solution)/shard_map/ppermute | solution.py:21
  415.2 24.7 %copy-start.5 = (f32[5,4,8,1152]{3,2,1,0:T(8,128)}, f32[5,4,8,1152]{3,2,1,0:T(8,128)S(1)}, u32[]{:S(2)}) copy-start(f32[5,4,8,1152]{3,2,1,0:T(8,128)S(1)} %fusion.88) | copy-start | bytes 2211844
  415.5 24.3 %collective-permute-start.8 = (f32[5,4,5,1152]{3,1,2,0:T(4,128)S(1)}, f32[5,4,5,1152]{3,1,2,0:T(4,128)S(1)}, u32[]{:S(2)}, u32[]{:S(2)}) collective-permute-start(f32[5,4,5,1152]{3,1,2,0:T(4,128)S(1)} %copy.193), channel_id=1, source_target_pairs={{0,1},{1,2},{2,3},{3,4},{4,5},{5,6},{6,7},{7,8},{8,9},{9,10},{10,1... | collective-permute-start | bytes 1382408 | tf_op jit(solution)/shard_map/ppermute | solution.py:21
  418.2 21.8 %copy-start.53 = (f32[10]{0:T(128)S(1)}, f32[10]{0:T(128)}, u32[]{:S(2)}) copy-start(f32[10]{0:T(128)} %get-tuple-element.207) | copy-start | bytes 124
  418.2 21.8 %copy-start.55 = (f32[10]{0:T(128)S(1)}, f32[10]{0:T(128)}, u32[]{:S(2)}) copy-start(f32[10]{0:T(128)} %get-tuple-element.208) | copy-start | bytes 124
  418.2 21.8 %copy-start.57 = (f32[10]{0:T(128)S(1)}, f32[10]{0:T(128)}, u32[]{:S(2)}) copy-start(f32[10]{0:T(128)} %get-tuple-element.209) | copy-start | bytes 124
  418.2 21.8 %copy-start.59 = (f32[10]{0:T(128)S(1)}, f32[10]{0:T(128)}, u32[]{:S(2)}) copy-start(f32[10]{0:T(128)} %get-tuple-element.210) | copy-start | bytes 124
  418.3 21.6 %collective-permute-start.9 = (f32[5,4,5,1152]{3,1,2,0:T(4,128)S(1)}, f32[5,4,5,1152]{3,1,2,0:T(4,128)S(1)}, u32[]{:S(2)}, u32[]{:S(2)}) collective-permute-start(f32[5,4,5,1152]{3,1,2,0:T(4,128)S(1)} %copy.195), channel_id=1, source_target_pairs={{1,0},{2,1},{3,2},{4,3},{5,4},{6,5},{7,6},{8,7},{9,8},{10,9},{11,1... | collective-permute-start | bytes 1382408 | tf_op jit(solution)/shard_map/ppermute | solution.py:23
  691.2 7.9 collective-permute-start.10
  697.2 6.8 collective-permute-start.11
  771.0 12.8 %collective-permute-start.12 = (f32[5,4,4,1152]{3,2,1,0:T(4,128)S(1)}, f32[5,4,4,1152]{3,2,1,0:T(4,128)S(1)}, u32[]{:S(2)}, u32[]{:S(2)}) collective-permute-start(f32[5,4,4,1152]{3,2,1,0:T(4,128)S(1)} %get-tuple-element.94), channel_id=1, source_target_pairs={{1,0},{2,1},{3,2},{4,3},{5,4},{6,5},{7,6},{8,7},{9,8},{10,9},{11,1... | collective-permute-start | bytes 1105928 | tf_op jit(solution)/shard_map/ppermute | solution.py:23
  773.1 18.5 %collective-permute-start.13 = (f32[5,4,4,1152]{3,2,1,0:T(4,128)S(1)}, f32[5,4,4,1152]{3,2,1,0:T(4,128)S(1)}, u32[]{:S(2)}, u32[]{:S(2)}) collective-permute-start(f32[5,4,4,1152]{3,2,1,0:T(4,128)S(1)} %get-tuple-element.95), channel_id=1, source_target_pairs={{0,1},{1,2},{2,3},{3,4},{4,5},{5,6},{6,7},{7,8},{8,9},{9,10},{10,1... | collective-permute-start | bytes 1105928 | tf_op jit(solution)/shard_map/ppermute | solution.py:21
  (62 other events, 649.4 us)
where the time goes:
time: 808 us; the launch traced here: 794 us
  local copies, waits for them, and re-layouts  258 us (32%)
  other arithmetic  229 us (28%)
  blocking collectives  153 us (19%)
  waiting for transfers between devices  77.4 us (10%)
  starting transfers between devices  64 us (8%)
  matrix products  8.2 us (1%)
    gather x6, local copies, waits for them, and re-layouts, body(): flat_tile[obs_points[slot_index]] - values[slot_index]  138 us
    scatter-add x6, other arithmetic, body(): jnp.zeros(flat_tile.shape, jnp.float32).at[obs_points[slot_index]]  133 us
    all_to_all x2, blocking collectives, from_everyone(): lax.all_to_all(jnp.broadcast_to(value[None], (count, *value.shape)), axis...  122 us
    another operation x12, local copies, waits for them, and re-layouts, fine_tile(): jnp.stack([even_cols, odd_cols], axis=-1)  49.9 us
    mul x6, other arithmetic, fine_tile(): odd_cols = 0.5 * (merid[..., :tile_half] + merid[..., 1:tile_half + 1])  40.8 us
    ppermute x7, waiting for transfers between devices, padded_2(): lax.ppermute(tail, axis, [(i, (i + 1) % count) for i in range(ends)])  33.4 us
    all_to_all x1, blocking collectives, sum_at_owner(): lax.all_to_all(blocks, axis, split_axis=0, concat_axis=0, tiled=True)  31.1 us
    ppermute x7, starting transfers between devices, padded_2(): lax.ppermute(tail, axis, [(i, (i + 1) % count) for i in range(ends)])  30.6 us
  transfers between devices with their start and end apart: 16, of which 8 were waited for; matrix products, arithmetic and copies ran while one was open for 3% of the time, Pallas kernels for 0%

commit v1 on v0

v1 whole, which is shorter than its diff:
```python
import functools

import jax
import jax.numpy as jnp
from jax import lax
from jax.experimental import pallas as pl
from jax.experimental.pallas import tpu as pltpu
from jax.sharding import PartitionSpec as P

MESH = pl.DeviceIdType.MESH
ITERS = 2
HALF = 4
STEP = 0.3
F32 = jnp.float32
BF16 = jnp.bfloat16


def column_chunks(width):
    return [(at, min(256, width - at)) for at in range(0, width, 256)]


def kernel(
    dims,
    alpha_h, mem_h, z_h, coef_h, idx_h, val_h, wgt_h, tile_s, count_s, out_h,
    cur, mem, z, coef, idx, val, wgt,
    edge_out, halo, xp, lhs, inc_out, inc_in, line_out, line_in,
    obs_acc, obs_out, obs_in, placed, planes, rim_out, rim_in,
    adj_out, adj_in, adj, wsum, zp, out_v,
    local_sem, halo_send, halo_recv, obs_send, obs_recv, rim_send, rim_recv,
    inc_send, inc_recv, line_send, line_recv, adj_send, adj_recv, w_send, w_recv,
):
    members, variables, levels, cols, n_mem, n_lat, slots, n_obs = dims
    kl_count, vl_count = members * levels, variables * levels
    lane_tiles, tiles = cols // 128, cols // 64
    m, b = lax.axis_index("mem"), lax.axis_index("lat")
    north, south = lax.rem(b + 1, n_lat), lax.rem(b + n_lat - 1, n_lat)
    h = lax.rem(m, 2)
    mate = m + 1 - 2 * h
    strip_north = dict(mem=mate, lat=lax.rem(b + h, n_lat))
    strip_south = dict(mem=mate, lat=lax.rem(b + h + n_lat - 1, n_lat))
    strip = 2 * b + h

    def remote(src, dst, send, recv, to):
        return pltpu.make_async_remote_copy(
            src_ref=src, dst_ref=dst, send_sem=send, recv_sem=recv, device_id=to, device_id_type=MESH
        )

    loads = [
        pltpu.make_async_copy(src, dst, local_sem.at[i])
        for i, (src, dst) in enumerate(
            ((alpha_h, cur), (coef_h, coef), (idx_h, idx), (val_h, val), (wgt_h, wgt), (z_h, z), (mem_h, mem))
        )
    ]
    for copy in loads:
        copy.start()

    barrier = pltpu.get_barrier_semaphore()

    @pl.loop(0, n_mem - 1)
    def _(i):
        pl.semaphore_signal(
            barrier, 1, device_id=dict(mem=lax.rem(m + 1 + i, n_mem), lat=b), device_id_type=MESH
        )

    for to in (
        dict(mem=m, lat=north),
        dict(mem=m, lat=south),
        dict(mem=mate, lat=lax.rem(b + 2 * h + n_lat - 1, n_lat)),
    ):
        pl.semaphore_signal(barrier, 1, device_id=to, device_id_type=MESH)

    loads[0].wait()

    @pl.loop(0, kl_count)
    def _(kl):
        edge_out[0, kl] = cur[kl, 0:4]
        edge_out[1, kl] = cur[kl, 4:8]

    pl.semaphore_wait(barrier, n_mem + 2)
    halo_copies = [
        remote(edge_out.at[0], halo.at[1], halo_send.at[0], halo_recv.at[1], dict(mem=m, lat=south)),
        remote(edge_out.at[1], halo.at[0], halo_send.at[1], halo_recv.at[0], dict(mem=m, lat=north)),
    ]
    for copy in halo_copies:
        copy.start()

    @pl.loop(0, kl_count)
    def _(kl):
        for j in range(lane_tiles):
            xp[kl, j, 4:12, :] = cur[kl, :, 128 * j : 128 * j + 128]

    for copy in loads[1:5]:
        copy.wait()

    hot_rows = 16 * vl_count
    width = min(512, n_obs)
    row_at = lax.broadcasted_iota(jnp.int32, (hot_rows, width), 0)
    col_at = lax.broadcasted_iota(jnp.int32, (128, width), 0)
    for slot in range(slots):
        obs_acc[...] = jnp.zeros_like(obs_acc)

        @pl.loop(0, n_obs // width)
        def _(step):
            start = pl.multiple_of(step * width, width)
            points = idx[slot : slot + 1, pl.ds(start, width)]
            place = lax.broadcasted_iota(jnp.int32, (1, width), 1) + start
            live = place < count_s[slot]
            weight = jnp.where(live, wgt[slot : slot + 1, pl.ds(start, width)], 0.0)
            scaled = weight * val[slot : slot + 1, pl.ds(start, width)]
            row = lax.shift_right_logical(points, 7)
            row = (row & ~7) + (row & 1) * 4 + (lax.shift_right_logical(row, 1) & 3)
            col = (points & 1) * 64 + lax.shift_right_logical(points & 127, 1)
            in_row = row_at == row
            parts = []
            for amount in (weight, scaled):
                high = amount.astype(BF16).astype(F32)
                for part in (high, amount - high):
                    parts.append(jnp.where(in_row, part, 0.0).astype(BF16))
            hot = jnp.where(col_at == col, 1.0, 0.0).astype(BF16)
            obs_acc[...] += lax.dot_general(
                jnp.concatenate(parts, axis=0), hot, (((1,), (1,)), ((), ())), preferred_element_type=F32
            )

        for q in range(2):
            both = obs_acc[2 * q * hot_rows : (2 * q + 1) * hot_rows, :] + obs_acc[
                (2 * q + 1) * hot_rows : (2 * q + 2) * hot_rows, :
            ]
            obs_out[:, q * slots + slot] = both.reshape(n_mem, 8, 128)

    sub = lax.broadcasted_iota(jnp.int32, (8, 128), 0)
    ids = jnp.full((8, 128), -1.0, F32)
    for slot in range(slots):
        ids = jnp.where(sub == slot, jnp.full((8, 128), tile_s[slot], jnp.int32).astype(F32), ids)
    for d in range(n_mem):
        obs_out[d, 2 * slots] = ids

    def to_peers(i):
        return lax.rem(m + 1 + i, n_mem)

    def obs_copy(i):
        peer = to_peers(i)
        return remote(
            obs_out.at[peer], obs_in.at[m], obs_send.at[peer], obs_recv.at[m], dict(mem=peer, lat=b)
        )

    def obs_wait(i):
        peer = to_peers(i)
        return remote(
            obs_out.at[peer], obs_in.at[peer], obs_send.at[peer], obs_recv.at[peer], dict(mem=peer, lat=b)
        )

    @pl.loop(0, n_mem - 1)
    def _(i):
        obs_copy(i).start()

    obs_in[m] = obs_out[m]

    block = coef[pl.ds(pl.multiple_of(b * 8, 8), 32), :]
    row8 = lax.broadcasted_iota(jnp.int32, (8, 128), 0) + b * 8

    def coef_rows(first, s):
        return jnp.broadcast_to(block[first : first + 8, s : s + 1], (8, 128))

    def forward_coefs():
        out = []
        for s in range(2 * HALF + 1):
            reach = row8 + (s - HALF)
            out.append(jnp.where((reach >= 0) & (reach < 8 * n_lat), coef_rows(8, s), 0.0))
        return out

    def adjoint_coefs(first):
        return [coef_rows(8 + first - (s - HALF), s) for s in range(2 * HALF + 1)]

    for copy in halo_copies:
        copy.wait()

    @pl.loop(0, kl_count)
    def _(kl):
        for j in range(lane_tiles):
            xp[kl, j, 0:4, :] = halo[0, kl, :, 128 * j : 128 * j + 128]
            xp[kl, j, 12:16, :] = halo[1, kl, :, 128 * j : 128 * j + 128]

    for it in range(ITERS):
        fc = forward_coefs()

        @pl.loop(0, kl_count // 2)
        def _(pair):
            for j in range(lane_tiles):
                both = []
                for e in range(2):
                    total = jnp.zeros((8, 128), F32)
                    for s in range(2 * HALF + 1):
                        total = total + fc[s] * xp[2 * pair + e, j, s : s + 8, :]
                    both.append(total)
                lhs[pl.ds(pl.multiple_of(pair * 16, 16), 16), 128 * j : 128 * j + 128] = jnp.concatenate(
                    both, axis=0
                ).astype(BF16)

        if it == 0:
            loads[5].wait()
            loads[6].wait()
        for at, size in column_chunks(cols):
            local = jnp.dot(lhs[...], z[:, at : at + size], preferred_element_type=F32)
            for vl in range(vl_count):
                level = vl % levels
                total = jnp.zeros((8, size), F32)
                for k in range(members):
                    first = (k * levels + level) * 8
                    total = total + mem[k * vl_count + vl, :, at : at + size].astype(F32) * local[first : first + 8]
                inc_out[it, 2 * vl, :, at : at + size] = total[0:4]
                inc_out[it, 2 * vl + 1, :, at : at + size] = total[4:8]

        def inc_copy(i, mine):
            peer = to_peers(i)
            return remote(
                inc_out.at[it, peer], inc_in.at[it, m if mine else peer], inc_send.at[it, peer],
                inc_recv.at[it, m if mine else peer], dict(mem=peer, lat=b),
            )

        @pl.loop(0, n_mem - 1)
        def _(i):
            inc_copy(i, True).start()

        inc_in[it, m] = inc_out[it, m]

        if it == 0:

            @pl.loop(0, n_mem - 1)
            def _(i):
                obs_wait(i).wait()

            @pl.loop(0, tiles)
            def _(t):
                wanted = jnp.full((8, 128), t, jnp.int32).astype(F32)
                w_total = jnp.zeros((8, 128), F32)
                v_total = jnp.zeros((8, 128), F32)
                for src in range(n_mem):
                    for slot in range(slots):
                        here = jnp.broadcast_to(obs_in[src, 2 * slots, slot : slot + 1, :], (8, 128)) == wanted
                        w_total = w_total + jnp.where(here, obs_in[src, slot], 0.0)
                        v_total = v_total + jnp.where(here, obs_in[src, slots + slot], 0.0)
                placed[t, 0] = w_total
                placed[t, 1] = v_total

            low = lax.broadcasted_iota(jnp.int32, (8, 128), 1) < 64
            for u in range(lane_tiles):
                for q in range(2):
                    first, second = placed[2 * u, q], placed[2 * u + 1, q]
                    lanes = slice(128 * u, 128 * u + 128)
                    planes[2 * q, 0:8, lanes] = jnp.where(low, first, pltpu.roll(second, 64, 1))
                    planes[2 * q + 1, 0:8, lanes] = jnp.where(low, pltpu.roll(first, 64, 1), second)
            for q in range(4):
                planes[q, 8:16, :] = jnp.zeros((8, cols), F32)
                rim_out[0, q : q + 1, :] = planes[q, 0:1, :]
                rim_out[1, q : q + 1, :] = planes[q, 7:8, :]
            rim_copies = [
                remote(rim_out.at[0], rim_in.at[1], rim_send.at[0], rim_recv.at[1], strip_south),
                remote(rim_out.at[1], rim_in.at[0], rim_send.at[1], rim_recv.at[0], strip_north),
            ]
            for copy in rim_copies:
                copy.start()

        @pl.loop(0, n_mem - 1)
        def _(i):
            inc_copy(i, False).wait()

        inc = inc_in[it, 0]
        for src in range(1, n_mem):
            inc = inc + inc_in[it, src]
        line_out[it, 0] = inc[0:1]
        line_out[it, 1] = inc[3:4]
        line_copies = [
            remote(line_out.at[it, 0], line_in.at[it, 1], line_send.at[it, 0], line_recv.at[it, 1], strip_south),
            remote(line_out.at[it, 1], line_in.at[it, 0], line_send.at[it, 1], line_recv.at[it, 0], strip_north),
        ]
        for copy in line_copies:
            copy.start()
        at_south = strip == 0
        at_north = strip == 2 * n_lat - 1
        if it == 0:
            for copy in rim_copies:
                copy.wait()
            for q in range(4):
                planes[q, 8:9, :] = jnp.where(at_south, 0.0, rim_in[0, q : q + 1, :])
                planes[q, 9:10, :] = jnp.where(at_north, 0.0, rim_in[1, q : q + 1, :])
        for copy in line_copies:
            copy.wait()
        below = jnp.where(at_south, inc[0:1], line_in[it, 0])
        above = jnp.where(at_north, inc[3:4], line_in[it, 1])
        fine = jnp.concatenate(
            [
                0.75 * inc + 0.25 * jnp.concatenate([below, inc[0:3]], axis=0),
                0.75 * inc + 0.25 * jnp.concatenate([inc[1:4], above], axis=0),
                0.75 * below + 0.25 * inc[0:1],
                0.75 * above + 0.25 * inc[3:4],
                jnp.zeros((6, cols), F32),
            ],
            axis=0,
        )
        odd = 0.5 * (fine + pltpu.roll(fine, cols - 1, 1))
        even_res = planes[0] * fine - planes[2]
        odd_res = planes[1] * odd - planes[3]
        back = even_res + 0.5 * (odd_res + pltpu.roll(odd_res, 1, 1))
        row_even, row_odd = back[0:4], back[4:8]
        strip_adj = 0.75 * (row_even + row_odd) + 0.25 * (
            jnp.concatenate([row_even[1:4], back[9:10]], axis=0)
            + jnp.concatenate([back[8:9], row_odd[0:3]], axis=0)
        )
        row4 = lax.broadcasted_iota(jnp.int32, (4, cols), 0)
        strip_adj = strip_adj + jnp.where(at_south & (row4 == 0), 0.25 * row_even, 0.0)
        strip_adj = strip_adj + jnp.where(at_north & (row4 == 3), 0.25 * row_odd, 0.0)
        adj_out[it] = strip_adj

        def adj_copy(i, mine):
            peer = to_peers(i)
            return remote(
                adj_out.at[it], adj_in.at[it, m if mine else peer], adj_send.at[it, peer],
                adj_recv.at[it, m if mine else peer], dict(mem=peer, lat=b),
            )

        @pl.loop(0, n_mem - 1)
        def _(i):
            adj_copy(i, True).start()

        adj_in[it, m] = strip_adj

        @pl.loop(0, n_mem - 1)
        def _(i):
            adj_copy(i, False).wait()

        for vl in range(vl_count):
            adj[vl, 0:4] = adj_in[it, 2 * vl]
            adj[vl, 4:8] = adj_in[it, 2 * vl + 1]

        @pl.loop(0, members)
        def _(k):
            for pair in range(levels // 2):
                for j in range(lane_tiles):
                    lanes = slice(128 * j, 128 * j + 128)
                    both = []
                    for level in (2 * pair, 2 * pair + 1):
                        total = jnp.zeros((8, 128), F32)
                        for v in range(variables):
                            vl = v * levels + level
                            total = total + mem[k * vl_count + vl, :, lanes].astype(F32) * adj[vl, :, lanes]
                        both.append(total)
                    first = pl.multiple_of(k * levels * 8 + pair * 16, 16)
                    wsum[it, 1, pl.ds(first, 16), lanes] = jnp.concatenate(both, axis=0).astype(BF16)

        w_copies = [
            remote(wsum.at[it, 1], wsum.at[it, 2], w_send.at[it, 0], w_recv.at[it, 1], dict(mem=m, lat=south)),
            remote(wsum.at[it, 1], wsum.at[it, 0], w_send.at[it, 1], w_recv.at[it, 0], dict(mem=m, lat=north)),
        ]
        for copy in w_copies:
            copy.start()

        def zonal_back(segment):
            for at, size in column_chunks(cols):
                part = lax.dot_general(
                    wsum[it, segment], z[at : at + size, :], (((1,), (1,)), ((), ())), preferred_element_type=F32
                )
                part = part.reshape(kl_count, 8, size)
                for e in range(size // 128):
                    zp[:, at // 128 + e, 8 * segment : 8 * segment + 8, :] = part[:, :, 128 * e : 128 * e + 128]

        zonal_back(1)
        for copy in w_copies:
            copy.wait()
        zonal_back(0)
        zonal_back(2)

        if it < ITERS - 1:
            for part in range(2):
                bc = adjoint_coefs(8 * part - 4)

                @pl.loop(0, kl_count)
                def _(kl):
                    for j in range(lane_tiles):
                        here = xp[kl, j, 8 * part : 8 * part + 8, :]
                        total = jnp.zeros((8, 128), F32)
                        for s in range(2 * HALF + 1):
                            first = 8 * part + 8 - s
                            total = total + bc[s] * zp[kl, j, first : first + 8, :]
                        xp[kl, j, 8 * part : 8 * part + 8, :] = here - STEP * (here + total)
        else:
            bc = adjoint_coefs(0)

            @pl.loop(0, kl_count)
            def _(kl):
                for j in range(lane_tiles):
                    here = xp[kl, j, 4:12, :]
                    total = jnp.zeros((8, 128), F32)
                    for s in range(2 * HALF + 1):
                        total = total + bc[s] * zp[kl, j, 12 - s : 20 - s, :]
                    out_v[kl, :, 128 * j : 128 * j + 128] = here - STEP * (here + total)

    store = pltpu.make_async_copy(out_v, out_h, local_sem.at[0])
    store.start()
    store.wait()


def body(n_mem, n_lat, members, alpha, zonal_loc, merid_coef, slot_tile, obs_count, obs_index, obs_value, obs_weight):
    k, v, l, rows, cols = members.shape
    slots, n_obs = obs_index.shape[2:]
    kl, vl, lane_tiles = k * l, v * l, cols // 128
    dims = (k, v, l, cols, n_mem, n_lat, slots, n_obs)
    coef = jnp.pad(merid_coef, ((8, 16), (0, 0)))
    vmem, dma = pltpu.VMEM, pltpu.SemaphoreType.DMA
    out = pl.pallas_call(
        functools.partial(kernel, dims),
        out_shape=jax.ShapeDtypeStruct((kl, rows, cols), F32),
        in_specs=[pl.BlockSpec(memory_space=pl.ANY)] * 7 + [pl.BlockSpec(memory_space=pltpu.SMEM)] * 2,
        out_specs=pl.BlockSpec(memory_space=pl.ANY),
        scratch_shapes=[
            vmem((kl, rows, cols), F32),
            vmem((k * vl, rows, cols), BF16),
            vmem((cols, cols), BF16),
            vmem(coef.shape, F32),
            vmem((slots, n_obs), jnp.int32),
            vmem((slots, n_obs), F32),
            vmem((slots, n_obs), F32),
            vmem((2, kl, 4, cols), F32),
            vmem((2, kl, 4, cols), F32),
            vmem((kl, lane_tiles, 16, 128), F32),
            vmem((kl * rows, cols), BF16),
            vmem((ITERS, n_mem, 4, cols), F32),
            vmem((ITERS, n_mem, 4, cols), F32),
            vmem((ITERS, 2, 1, cols), F32),
            vmem((ITERS, 2, 1, cols), F32),
            vmem((64 * vl, 128), F32),
            vmem((n_mem, 2 * slots + 1, 8, 128), F32),
            vmem((n_mem, 2 * slots + 1, 8, 128), F32),
            vmem((2 * lane_tiles, 2, 8, 128), F32),
            vmem((4, 16, cols), F32),
            vmem((2, 4, cols), F32),
            vmem((2, 4, cols), F32),
            vmem((ITERS, 4, cols), F32),
            vmem((ITERS, n_mem, 4, cols), F32),
            vmem((vl, 8, cols), F32),
            vmem((ITERS, 3, kl * rows, cols), BF16),
            vmem((kl, lane_tiles, 24, 128), F32),
            vmem((kl, rows, cols), F32),
            dma((7,)),
            dma((2,)), dma((2,)),
            dma((n_mem,)), dma((n_mem,)),
            dma((2,)), dma((2,)),
            dma((ITERS, n_mem)), dma((ITERS, n_mem)),
            dma((ITERS, 2)), dma((ITERS, 2)),
            dma((ITERS, n_mem)), dma((ITERS, n_mem)),
            dma((ITERS, 2)), dma((ITERS, 2)),
        ],
        compiler_params=pltpu.CompilerParams(
            collective_id=0, has_side_effects=True, vmem_limit_bytes=60 * 1024 * 1024
        ),
    )(
        alpha.reshape(kl, rows, cols),
        members.reshape(k * vl, rows, cols),
        zonal_loc,
        coef,
        obs_index.reshape(slots, n_obs),
        obs_value.reshape(slots, n_obs),
        obs_weight.reshape(slots, n_obs),
        slot_tile.reshape(slots),
        obs_count.reshape(slots),
    )
    return out.reshape(alpha.shape)


def solution(mesh):
    in_specs = (
        P("mem", None, None, "lat", None),
        P("mem", None, "lat", None),
        P(),
        P(),
        P("lat", "mem", None),
        P("lat", "mem", None),
        P("lat", "mem", None, None),
        P("lat", "mem", None, None),
        P("lat", "mem", None, None),
    )
    step = functools.partial(body, mesh.shape["mem"], mesh.shape["lat"])
    return jax.shard_map(step, mesh=mesh, in_specs=in_specs, out_specs=P("mem", None, "lat", None), check_vma=False)
```

time: 808 us -> 119 us (0.15); the launches traced: 794 us -> 119 us
  local copies, waits for them, and re-layouts: 258 us -> 6.46 us
  other arithmetic: 229 us -> 0 us
  blocking collectives: 153 us -> 0 us
  Pallas kernels: 0 us -> 113 us
  waiting for transfers between devices: 77.4 us -> 0 us
  starting transfers between devices: 64 us -> 0 us
  matrix products: 8.2 us -> 0 us
    all_to_all x3 -> x0, blocking collectives: 153 us -> none  [the longest x2 122 us: from_everyone(): lax.all_to_all(jnp.broadcast_to(value[None], (count, *value.shape)), axis...]
    gather x8 -> x0, local copies, waits for them, and re-layouts: 144 us -> none  [the longest x6 138 us: body(): flat_tile[obs_points[slot_index]] - values[slot_index]]
    scatter-add x6 -> x0, other arithmetic: 133 us -> none  [body(): jnp.zeros(flat_tile.shape, jnp.float32).at[obs_points[slot_index]]]
    pallas_call x0 -> x1, Pallas kernels: none -> 113 us  [body(): pl.pallas_call(functools.partial(kernel, dims), out_shape=jax.ShapeDtypeS...]
    ppermute x14 -> x0, waiting for transfers between devices: 52 us -> none  [the longest x7 33.4 us: padded_2(): lax.ppermute(tail, axis, [(i, (i + 1) % count) for i in range(ends)])]
    another operation x27 -> x0, local copies, waits for them, and re-layouts: 51.9 us -> none  [the longest x12 49.9 us: fine_tile(): jnp.stack([even_cols, odd_cols], axis=-1)]
    ppermute x14 -> x0, starting transfers between devices: 50 us -> none  [the longest x7 30.6 us: padded_2(): lax.ppermute(tail, axis, [(i, (i + 1) % count) for i in range(ends)])]
    mul x17 -> x0, other arithmetic: 45.8 us -> none  [the longest x6 40.8 us: fine_tile(): odd_cols = 0.5 * (merid[..., :tile_half] + merid[..., 1:tile_half + 1])]
  transfers between devices with their start and end apart: 16 -> 0, of which waited for: 8 -> 0; matrix products, arithmetic and copies ran while one was open for 3% -> 0% of each run, Pallas kernels for 0% -> 0%
where the time goes in v1:
time: 119 us
  Pallas kernels  113 us (95%)
  local copies, waits for them, and re-layouts  6.46 us (5%)
    pallas_call x1, Pallas kernels, body(): pl.pallas_call(functools.partial(kernel, dims), out_shape=jax.ShapeDtypeS...  113 us
    unnamed x4, local copies, waits for them, and re-layouts  5.82 us

profile of v1, /device:TPU:2, one launch (start us, length us, event | category | flops | bytes accessed | tf_op | source)
XLA Modules:
  0.0 119.1 jit_solution(9941789818148078985)
XLA Ops:
  0.0 0.8 copy.10
  0.8 0.6 pad.4.coef_h
  1.4 1.4 %copy.17 = s32[1,1,3,4096]{3,2,1,0:T(4,128)} copy(s32[1,1,3,4096]{3,1,2,0:T(1,128)} %param.15) | data formatting | bytes 98304
  2.9 1.5 %copy_bitcast_fusion = (f32[3,4096]{1,0:T(4,128)}, f32[3,4096]{1,0:T(4,128)}) fusion(f32[1,1,3,4096]{3,1,2,0:T(1,128)} %param.17, f32[1,1,3,4096]{3,1,2,0:T(1,128)} %param.16), kind=kLoop, calls=%fused_computation | loop fusion | bytes 196608
  4.4 112.6 %shard_map.91 = f32[20,8,1152]{2,1,0:T(8,128)} custom-call(f32[20,8,1152]{2,1,0:T(8,128)} %bitcast.13, bf16[40,8,1152]{2,1,0:T(8,128)(2,1)} %bitcast.14, bf16[1152,1152]{1,0:T(8,128)(2,1)} %z_h.1, f32[152,9]{1,0:T(8,128)} %pad.4.coef_h, s32[3,4096]{1,0:T(4,128)} %bitcast.15, f32[3,4096]{1,0:T(4,128)} %get-tuple-element.6.val_h, ...), custom_call_target="tpu_custom_call" | custom-call | tf_op jit(solution)/shard_map/pallas_call | solution.py:409
  117.0 2.0 %copy.19 = f32[5,4,8,1152]{3,2,1,0:T(8,128)} copy(f32[5,4,8,1152]{3,2,1,0:T(8,128)} %bitcast.12) | data formatting | bytes 1474560

commit v2 on v1

--- a/solution.py
+++ b/solution.py
@@ -22,15 +22,16 @@
 def kernel(
     dims,
     alpha_h, mem_h, z_h, coef_h, idx_h, val_h, wgt_h, tile_s, count_s, out_h,
-    cur, mem, z, coef, idx, val, wgt,
+    cur, mem, z, coef_in, coef, idx, val, wgt,
     edge_out, halo, xp, lhs, inc_out, inc_in, line_out, line_in,
     obs_acc, obs_out, obs_in, placed, planes, rim_out, rim_in,
-    adj_out, adj_in, adj, wsum, zp, out_v,
-    local_sem, halo_send, halo_recv, obs_send, obs_recv, rim_send, rim_recv,
+    adj_out, adj_in, adj, w_out, w_in, w_in_last, zp, out_v,
+    local_sem, store_sem, halo_send, halo_recv, obs_send, obs_recv, rim_send, rim_recv,
     inc_send, inc_recv, line_send, line_recv, adj_send, adj_recv, w_send, w_recv,
 ):
     members, variables, levels, cols, n_mem, n_lat, slots, n_obs = dims
     kl_count, vl_count = members * levels, variables * levels
+    k_rows = levels * 8
     lane_tiles, tiles = cols // 128, cols // 64
     m, b = lax.axis_index("mem"), lax.axis_index("lat")
     north, south = lax.rem(b + 1, n_lat), lax.rem(b + n_lat - 1, n_lat)
@@ -48,11 +49,15 @@
     loads = [
         pltpu.make_async_copy(src, dst, local_sem.at[i])
         for i, (src, dst) in enumerate(
-            ((alpha_h, cur), (coef_h, coef), (idx_h, idx), (val_h, val), (wgt_h, wgt), (z_h, z), (mem_h, mem))
+            ((alpha_h, cur), (coef_h, coef_in), (idx_h, idx), (val_h, val), (wgt_h, wgt), (z_h, z), (mem_h, mem))
         )
     ]
     for copy in loads:
         copy.start()
+
+    def store(k):
+        part = pl.ds(k * levels, levels)
+        return pltpu.make_async_copy(out_v.at[part], out_h.at[part], store_sem.at[k])
 
     barrier = pltpu.get_barrier_semaphore()
 
@@ -77,12 +82,22 @@
         edge_out[1, kl] = cur[kl, 4:8]
 
     pl.semaphore_wait(barrier, n_mem + 2)
-    halo_copies = [
-        remote(edge_out.at[0], halo.at[1], halo_send.at[0], halo_recv.at[1], dict(mem=m, lat=south)),
-        remote(edge_out.at[1], halo.at[0], halo_send.at[1], halo_recv.at[0], dict(mem=m, lat=north)),
-    ]
-    for copy in halo_copies:
-        copy.start()
+
+    def halo_copies(k):
+        part = pl.ds(k * levels, levels)
+        return [
+            remote(
+                edge_out.at[0, part], halo.at[1, part], halo_send.at[0, k], halo_recv.at[1, k], dict(mem=m, lat=south)
+            ),
+            remote(
+                edge_out.at[1, part], halo.at[0, part], halo_send.at[1, k], halo_recv.at[0, k], dict(mem=m, lat=north)
+            ),
+        ]
+
+    @pl.loop(0, members)
+    def _(k):
+        for copy in halo_copies(k):
+            copy.start()
 
     @pl.loop(0, kl_count)
     def _(kl):
@@ -102,11 +117,11 @@
         @pl.loop(0, n_obs // width)
         def _(step):
             start = pl.multiple_of(step * width, width)
-            points = idx[slot : slot + 1, pl.ds(start, width)]
+            points = idx[slot, :, pl.ds(start, width)]
             place = lax.broadcasted_iota(jnp.int32, (1, width), 1) + start
             live = place < count_s[slot]
-            weight = jnp.where(live, wgt[slot : slot + 1, pl.ds(start, width)], 0.0)
-            scaled = weight * val[slot : slot + 1, pl.ds(start, width)]
+            weight = jnp.where(live, wgt[slot, :, pl.ds(start, width)], 0.0)
+            scaled = weight * val[slot, :, pl.ds(start, width)]
             row = lax.shift_right_logical(points, 7)
             row = (row & ~7) + (row & 1) * 4 + (lax.shift_right_logical(row, 1) & 3)
             col = (points & 1) * 64 + lax.shift_right_logical(points & 127, 1)
@@ -155,6 +170,11 @@
 
     obs_in[m] = obs_out[m]
 
+    grid_rows, taps = coef_in.shape[1], coef_in.shape[0]
+    coef[...] = jnp.zeros_like(coef)
+    coef[8 : 8 + grid_rows, :] = jnp.concatenate(
+        [coef_in[...], jnp.zeros((128 - taps, grid_rows), F32)], axis=0
+    ).T
     block = coef[pl.ds(pl.multiple_of(b * 8, 8), 32), :]
     row8 = lax.broadcasted_iota(jnp.int32, (8, 128), 0) + b * 8
 
@@ -171,31 +191,37 @@
     def adjoint_coefs(first):
         return [coef_rows(8 + first - (s - HALF), s) for s in range(2 * HALF + 1)]
 
-    for copy in halo_copies:
-        copy.wait()
-
-    @pl.loop(0, kl_count)
-    def _(kl):
-        for j in range(lane_tiles):
-            xp[kl, j, 0:4, :] = halo[0, kl, :, 128 * j : 128 * j + 128]
-            xp[kl, j, 12:16, :] = halo[1, kl, :, 128 * j : 128 * j + 128]
-
-    for it in range(ITERS):
+    def spread_rows(k):
         fc = forward_coefs()
 
-        @pl.loop(0, kl_count // 2)
+        @pl.loop(0, levels // 2)
         def _(pair):
             for j in range(lane_tiles):
                 both = []
                 for e in range(2):
                     total = jnp.zeros((8, 128), F32)
                     for s in range(2 * HALF + 1):
-                        total = total + fc[s] * xp[2 * pair + e, j, s : s + 8, :]
+                        total = total + fc[s] * xp[k * levels + 2 * pair + e, j, s : s + 8, :]
                     both.append(total)
-                lhs[pl.ds(pl.multiple_of(pair * 16, 16), 16), 128 * j : 128 * j + 128] = jnp.concatenate(
-                    both, axis=0
-                ).astype(BF16)
-
+                first = pl.multiple_of(k * k_rows + pair * 16, 16)
+                lhs[pl.ds(first, 16), 128 * j : 128 * j + 128] = jnp.concatenate(both, axis=0).astype(BF16)
+
+    @pl.loop(0, members)
+    def _(k):
+        for copy in halo_copies(k):
+            copy.wait()
+
+        @pl.loop(0, levels)
+        def _(level):
+            kl = k * levels + level
+            for j in range(lane_tiles):
+                xp[kl, j, 0:4, :] = halo[0, kl, :, 128 * j : 128 * j + 128]
+                xp[kl, j, 12:16, :] = halo[1, kl, :, 128 * j : 128 * j + 128]
+
+        spread_rows(k)
+
+    for it in range(ITERS):
+        last = it == ITERS - 1
         if it == 0:
             loads[5].wait()
             loads[6].wait()
@@ -332,71 +358,110 @@
             adj[vl, 0:4] = adj_in[it, 2 * vl]
             adj[vl, 4:8] = adj_in[it, 2 * vl + 1]
 
+        w_from = w_in_last if last else w_in
+
+        def w_copies(k):
+            lower, upper = (w_out.at[it, k, 0:16], w_out.at[it, k, 16:32]) if last else (w_out.at[it, k],) * 2
+            half = lower.shape[0]
+            return [
+                remote(
+                    lower, w_from.at[k, half : 2 * half], w_send.at[it, 0, k], w_recv.at[it, 1, k],
+                    dict(mem=m, lat=south),
+                ),
+                remote(
+                    upper, w_from.at[k, 0:half], w_send.at[it, 1, k], w_recv.at[it, 0, k], dict(mem=m, lat=north)
+                ),
+            ]
+
         @pl.loop(0, members)
         def _(k):
-            for pair in range(levels // 2):
-                for j in range(lane_tiles):
-                    lanes = slice(128 * j, 128 * j + 128)
-                    both = []
-                    for level in (2 * pair, 2 * pair + 1):
-                        total = jnp.zeros((8, 128), F32)
-                        for v in range(variables):
-                            vl = v * levels + level
-                            total = total + mem[k * vl_count + vl, :, lanes].astype(F32) * adj[vl, :, lanes]
-                        both.append(total)
-                    first = pl.multiple_of(k * levels * 8 + pair * 16, 16)
-                    wsum[it, 1, pl.ds(first, 16), lanes] = jnp.concatenate(both, axis=0).astype(BF16)
-
-        w_copies = [
-            remote(wsum.at[it, 1], wsum.at[it, 2], w_send.at[it, 0], w_recv.at[it, 1], dict(mem=m, lat=south)),
-            remote(wsum.at[it, 1], wsum.at[it, 0], w_send.at[it, 1], w_recv.at[it, 0], dict(mem=m, lat=north)),
-        ]
-        for copy in w_copies:
-            copy.start()
-
-        def zonal_back(segment):
+            for j in range(lane_tiles):
+                lanes = slice(128 * j, 128 * j + 128)
+                rows = []
+                for level in range(levels):
+                    total = jnp.zeros((8, 128), F32)
+                    for v in range(variables):
+                        vl = v * levels + level
+                        total = total + mem[k * vl_count + vl, :, lanes].astype(F32) * adj[vl, :, lanes]
+                    rows.append(total)
+                if last:
+                    rows = [r[0:4] for r in rows] + [r[4:8] for r in rows]
+                w_out[it, k, :, lanes] = jnp.concatenate(rows, axis=0).astype(BF16)
+            for copy in w_copies(k):
+                copy.start()
+
+        def zonal_product(rows, store):
             for at, size in column_chunks(cols):
                 part = lax.dot_general(
-                    wsum[it, segment], z[at : at + size, :], (((1,), (1,)), ((), ())), preferred_element_type=F32
+                    rows, z[at : at + size, :], (((1,), (1,)), ((), ())), preferred_element_type=F32
                 )
-                part = part.reshape(kl_count, 8, size)
                 for e in range(size // 128):
-                    zp[:, at // 128 + e, 8 * segment : 8 * segment + 8, :] = part[:, :, 128 * e : 128 * e + 128]
-
-        zonal_back(1)
-        for copy in w_copies:
-            copy.wait()
-        zonal_back(0)
-        zonal_back(2)
-
-        if it < ITERS - 1:
-            for part in range(2):
-                bc = adjoint_coefs(8 * part - 4)
-
-                @pl.loop(0, kl_count)
-                def _(kl):
+                    store(at // 128 + e, part[:, 128 * e : 128 * e + 128])
+
+        def own_rows(j, part):
+            for k in range(members):
+                for level in range(levels):
+                    kl, first = k * levels + level, k * k_rows
+                    if last:
+                        zp[kl, j, 8:12, :] = part[first + 4 * level : first + 4 * level + 4]
+                        first += k_rows // 2
+                        zp[kl, j, 12:16, :] = part[first + 4 * level : first + 4 * level + 4]
+                    else:
+                        zp[kl, j, 8:16, :] = part[first + 8 * level : first + 8 * level + 8]
+
+        zonal_product(w_out[it].reshape(members * k_rows, cols), own_rows)
+
+        coefs = [adjoint_coefs(0)] if last else [adjoint_coefs(-4), adjoint_coefs(4)]
+
+        @pl.loop(0, members)
+        def _(k):
+            for copy in w_copies(k):
+                copy.wait()
+
+            def neighbour_rows(j, part):
+                for level in range(levels):
+                    kl = k * levels + level
+                    if last:
+                        zp[kl, j, 4:8, :] = part[4 * level : 4 * level + 4]
+                        zp[kl, j, 16:20, :] = part[16 + 4 * level : 20 + 4 * level]
+                    else:
+                        zp[kl, j, 0:8, :] = part[8 * level : 8 * level + 8]
+                        zp[kl, j, 16:24, :] = part[k_rows + 8 * level : k_rows + 8 * level + 8]
+
+            zonal_product(w_from[k], neighbour_rows)
+
+            if last:
+
+                @pl.loop(0, levels)
+                def _(level):
+                    kl = k * levels + level
                     for j in range(lane_tiles):
-                        here = xp[kl, j, 8 * part : 8 * part + 8, :]
+                        here = xp[kl, j, 4:12, :]
                         total = jnp.zeros((8, 128), F32)
                         for s in range(2 * HALF + 1):
-                            first = 8 * part + 8 - s
-                            total = total + bc[s] * zp[kl, j, first : first + 8, :]
-                        xp[kl, j, 8 * part : 8 * part + 8, :] = here - STEP * (here + total)
-        else:
-            bc = adjoint_coefs(0)
-
-            @pl.loop(0, kl_count)
-            def _(kl):
-                for j in range(lane_tiles):
-                    here = xp[kl, j, 4:12, :]
-                    total = jnp.zeros((8, 128), F32)
-                    for s in range(2 * HALF + 1):
-                        total = total + bc[s] * zp[kl, j, 12 - s : 20 - s, :]
-                    out_v[kl, :, 128 * j : 128 * j + 128] = here - STEP * (here + total)
-
-    store = pltpu.make_async_copy(out_v, out_h, local_sem.at[0])
-    store.start()
-    store.wait()
+                            total = total + coefs[0][s] * zp[kl, j, 12 - s : 20 - s, :]
+                        out_v[kl, :, 128 * j : 128 * j + 128] = here - STEP * (here + total)
+
+                store(k).start()
+            else:
+                for part in range(2):
+
+                    @pl.loop(0, levels)
+                    def _(level):
+                        kl = k * levels + level
+                        for j in range(lane_tiles):
+                            here = xp[kl, j, 8 * part : 8 * part + 8, :]
+                            total = jnp.zeros((8, 128), F32)
+                            for s in range(2 * HALF + 1):
+                                first = 8 * part + 8 - s
+                                total = total + coefs[part][s] * zp[kl, j, first : first + 8, :]
+                            xp[kl, j, 8 * part : 8 * part + 8, :] = here - STEP * (here + total)
+
+                spread_rows(k)
+
+    @pl.loop(0, members)
+    def _(k):
+        store(k).wait()
 
 
 def body(n_mem, n_lat, members, alpha, zonal_loc, merid_coef, slot_tile, obs_count, obs_index, obs_value, obs_weight):
@@ -404,8 +469,12 @@
     slots, n_obs = obs_index.shape[2:]
     kl, vl, lane_tiles = k * l, v * l, cols // 128
     dims = (k, v, l, cols, n_mem, n_lat, slots, n_obs)
-    coef = jnp.pad(merid_coef, ((8, 16), (0, 0)))
+    n_taps = merid_coef.shape[1]
     vmem, dma = pltpu.VMEM, pltpu.SemaphoreType.DMA
+
+    def by_slot(array):
+        return array.transpose(0, 2, 1, 3).reshape(slots, 1, n_obs)
+
     out = pl.pallas_call(
         functools.partial(kernel, dims),
         out_shape=jax.ShapeDtypeStruct((kl, rows, cols), F32),
@@ -415,10 +484,11 @@
             vmem((kl, rows, cols), F32),
             vmem((k * vl, rows, cols), BF16),
             vmem((cols, cols), BF16),
-            vmem(coef.shape, F32),
-            vmem((slots, n_obs), jnp.int32),
-            vmem((slots, n_obs), F32),
-            vmem((slots, n_obs), F32),
+            vmem((n_taps, n_lat * rows), F32),
+            vmem((n_lat * rows + 24, 128), F32),
+            vmem((slots, 1, n_obs), jnp.int32),
+            vmem((slots, 1, n_obs), F32),
+            vmem((slots, 1, n_obs), F32),
             vmem((2, kl, 4, cols), F32),
             vmem((2, kl, 4, cols), F32),
             vmem((kl, lane_tiles, 16, 128), F32),
@@ -437,17 +507,19 @@
             vmem((ITERS, 4, cols), F32),
             vmem((ITERS, n_mem, 4, cols), F32),
             vmem((vl, 8, cols), F32),
-            vmem((ITERS, 3, kl * rows, cols), BF16),
+            vmem((ITERS, k, l * rows, cols), BF16),
+            vmem((k, 2 * l * rows, cols), BF16),
+            vmem((k, l * rows, cols), BF16),
             vmem((kl, lane_tiles, 24, 128), F32),
             vmem((kl, rows, cols), F32),
-            dma((7,)),
-            dma((2,)), dma((2,)),
+            dma((7,)), dma((k,)),
+            dma((2, k)), dma((2, k)),
             dma((n_mem,)), dma((n_mem,)),
             dma((2,)), dma((2,)),
             dma((ITERS, n_mem)), dma((ITERS, n_mem)),
             dma((ITERS, 2)), dma((ITERS, 2)),
             dma((ITERS, n_mem)), dma((ITERS, n_mem)),
-            dma((ITERS, 2)), dma((ITERS, 2)),
+            dma((ITERS, 2, k)), dma((ITERS, 2, k)),
         ],
         compiler_params=pltpu.CompilerParams(
             collective_id=0, has_side_effects=True, vmem_limit_bytes=60 * 1024 * 1024
@@ -456,10 +528,10 @@
         alpha.reshape(kl, rows, cols),
         members.reshape(k * vl, rows, cols),
         zonal_loc,
-        coef,
-        obs_index.reshape(slots, n_obs),
-        obs_value.reshape(slots, n_obs),
-        obs_weight.reshape(slots, n_obs),
+        merid_coef.T,
+        by_slot(obs_index),
+        by_slot(obs_value),
+        by_slot(obs_weight),
         slot_tile.reshape(slots),
         obs_count.reshape(slots),
     )

time: 119 us -> 103 us (0.87)
  Pallas kernels: 113 us -> 101 us
  local copies, waits for them, and re-layouts: 6.46 us -> 2.03 us
    pallas_call x1, Pallas kernels: 113 us -> 101 us  [body(): pl.pallas_call(functools.partial(kernel, dims), out_shape=jax.ShapeDtypeS...]
    unnamed x4 -> x1, local copies, waits for them, and re-layouts: 5.82 us -> 2.03 us
where the time goes in v2:
time: 103 us
  Pallas kernels  101 us (98%)
  local copies, waits for them, and re-layouts  2.03 us (2%)
    pallas_call x1, Pallas kernels, body(): pl.pallas_call(functools.partial(kernel, dims), out_shape=jax.ShapeDtypeS...  101 us

profile of v2, /device:TPU:2, one launch (start us, length us, event | category | flops | bytes accessed | tf_op | source)
XLA Modules:
  0.0 102.6 jit_solution(1757119666597713711)
XLA Ops:
  0.0 100.5 %shard_map.91 = f32[20,8,1152]{2,1,0:T(8,128)} custom-call(f32[20,8,1152]{2,1,0:T(8,128)} %bitcast.10, bf16[40,8,1152]{2,1,0:T(8,128)(2,1)} %bitcast.11, bf16[1152,1152]{1,0:T(8,128)(2,1)} %z_h.1, f32[9,128]{1,0:T(8,128)} %bitcast.15, s32[3,1,4096]{2,1,0:T(1,128)} %bitcast.12, f32[3,1,4096]{2,1,0:T(1,128)} %bitcast.13, f32[3,1,4096]{2,1,0:T(1,128)} %bitcast.14, ...), custom_call_target="tpu_custom_call" | custom-call | tf_op jit(solution)/shard_map/pallas_call | solution.py:478
  100.5 2.0 %copy.11 = f32[5,4,8,1152]{3,2,1,0:T(8,128)} copy(f32[5,4,8,1152]{3,2,1,0:T(8,128)} %bitcast.9) | data formatting | bytes 1474560

commit v3 on v2

--- a/solution.py
+++ b/solution.py
@@ -22,7 +22,7 @@
 def kernel(
     dims,
     alpha_h, mem_h, z_h, coef_h, idx_h, val_h, wgt_h, tile_s, count_s, out_h,
-    cur, mem, z, coef_in, coef, idx, val, wgt,
+    cur, mem, z, z_t, coef_in, coef, idx, val, wgt,
     edge_out, halo, xp, lhs, inc_out, inc_in, line_out, line_in,
     obs_acc, obs_out, obs_in, placed, planes, rim_out, rim_in,
     adj_out, adj_in, adj, w_out, w_in, w_in_last, zp, out_v,
@@ -37,6 +37,18 @@
     north, south = lax.rem(b + 1, n_lat), lax.rem(b + n_lat - 1, n_lat)
     h = lax.rem(m, 2)
     mate = m + 1 - 2 * h
+    group = n_mem // 2
+    x_half = lax.rem(lax.div(m, 2), 2)
+    spot = lax.div(m, 4) * 2 + h
+    across = m + 2 - 4 * x_half
+
+    def near(i):
+        other = lax.rem(spot + 1 + i, group)
+        return other, lax.div(other, 2) * 4 + x_half * 2 + lax.rem(other, 2)
+
+    def far(peer):
+        return peer + 2 - 4 * x_half
+
     strip_north = dict(mem=mate, lat=lax.rem(b + h, n_lat))
     strip_south = dict(mem=mate, lat=lax.rem(b + h + n_lat - 1, n_lat))
     strip = 2 * b + h
@@ -170,6 +182,10 @@
 
     obs_in[m] = obs_out[m]
 
+    loads[5].wait()
+    for at, size in column_chunks(cols):
+        z_t[:, at : at + size] = z[at : at + size, :].T
+
     grid_rows, taps = coef_in.shape[1], coef_in.shape[0]
     coef[...] = jnp.zeros_like(coef)
     coef[8 : 8 + grid_rows, :] = jnp.concatenate(
@@ -223,7 +239,6 @@
     for it in range(ITERS):
         last = it == ITERS - 1
         if it == 0:
-            loads[5].wait()
             loads[6].wait()
         for at, size in column_chunks(cols):
             local = jnp.dot(lhs[...], z[:, at : at + size], preferred_element_type=F32)
@@ -337,22 +352,39 @@
         strip_adj = strip_adj + jnp.where(at_north & (row4 == 3), 0.25 * row_odd, 0.0)
         adj_out[it] = strip_adj
 
-        def adj_copy(i, mine):
-            peer = to_peers(i)
+        def adj_copy(i, owner, mine):
+            peer = near(i)[1]
+            own = owner == 0
+            mark = (m if own else across) if mine else (peer if own else far(peer))
             return remote(
-                adj_out.at[it], adj_in.at[it, m if mine else peer], adj_send.at[it, peer],
-                adj_recv.at[it, m if mine else peer], dict(mem=peer, lat=b),
+                adj_out.at[it] if own else adj_in.at[it, across], adj_in.at[it, mark],
+                adj_send.at[it, peer if own else far(peer)], adj_recv.at[it, mark], dict(mem=peer, lat=b),
             )
 
-        @pl.loop(0, n_mem - 1)
+        def cross_copy(mark):
+            return remote(
+                adj_out.at[it], adj_in.at[it, mark], adj_send.at[it, across], adj_recv.at[it, mark],
+                dict(mem=across, lat=b),
+            )
+
+        cross_copy(m).start()
+
+        @pl.loop(0, group - 1)
         def _(i):
-            adj_copy(i, True).start()
+            adj_copy(i, 0, True).start()
 
         adj_in[it, m] = strip_adj
-
-        @pl.loop(0, n_mem - 1)
+        cross_copy(across).wait()
+
+        @pl.loop(0, group - 1)
         def _(i):
-            adj_copy(i, False).wait()
+            adj_copy(i, 1, True).start()
+
+        for owner in range(2):
+
+            @pl.loop(0, group - 1)
+            def _(i):
+                adj_copy(i, owner, False).wait()
 
         for vl in range(vl_count):
             adj[vl, 0:4] = adj_in[it, 2 * vl]
@@ -392,9 +424,7 @@
 
         def zonal_product(rows, store):
             for at, size in column_chunks(cols):
-                part = lax.dot_general(
-                    rows, z[at : at + size, :], (((1,), (1,)), ((), ())), preferred_element_type=F32
-                )
+                part = jnp.dot(rows, z_t[:, at : at + size], preferred_element_type=F32)
                 for e in range(size // 128):
                     store(at // 128 + e, part[:, 128 * e : 128 * e + 128])
 
@@ -483,6 +513,7 @@
         scratch_shapes=[
             vmem((kl, rows, cols), F32),
             vmem((k * vl, rows, cols), BF16),
+            vmem((cols, cols), BF16),
             vmem((cols, cols), BF16),
             vmem((n_taps, n_lat * rows), F32),
             vmem((n_lat * rows + 24, 128), F32),

time: 103 us -> 98.4 us (0.955)
  Pallas kernels: 101 us -> 96.2 us
    pallas_call x1, Pallas kernels: 101 us -> 96.2 us  [body(): pl.pallas_call(functools.partial(kernel, dims), out_shape=jax.ShapeDtypeS...]
where the time goes in v3:
time: 98.4 us; the launch traced here: 98.3 us
  Pallas kernels  96.2 us (98%)
  local copies, waits for them, and re-layouts  2.03 us (2%)
    pallas_call x1, Pallas kernels, body(): pl.pallas_call(functools.partial(kernel, dims), out_shape=jax.ShapeDtypeS...  96.2 us
    unnamed x1, local copies, waits for them, and re-layouts  2.03 us

profile of v3, /device:TPU:2, one launch (start us, length us, event | category | flops | bytes accessed | tf_op | source)
XLA Modules:
  0.0 98.3 jit_solution(2535889804383610681)
XLA Ops:
  0.0 96.2 %shard_map.91 = f32[20,8,1152]{2,1,0:T(8,128)} custom-call(f32[20,8,1152]{2,1,0:T(8,128)} %bitcast.10, bf16[40,8,1152]{2,1,0:T(8,128)(2,1)} %bitcast.11, bf16[1152,1152]{1,0:T(8,128)(2,1)} %z_h.1, f32[9,128]{1,0:T(8,128)} %bitcast.15, s32[3,1,4096]{2,1,0:T(1,128)} %bitcast.12, f32[3,1,4096]{2,1,0:T(1,128)} %bitcast.13, f32[3,1,4096]{2,1,0:T(1,128)} %bitcast.14, ...), custom_call_target="tpu_custom_call" | custom-call | tf_op jit(solution)/shard_map/pallas_call | solution.py:508
  96.2 2.0 %copy.11 = f32[5,4,8,1152]{3,2,1,0:T(8,128)} copy(f32[5,4,8,1152]{3,2,1,0:T(8,128)} %bitcast.9) | data formatting | bytes 1474560
